TPU v7x, 512 devices: a whole 4x4x16 slice. The times are simulated.
512 devices in a mesh: wide: 64 (over z_hi, y, x, core), narrow: 8 (over z_lo).
Axes of the slice: x: 4, y: 4, z: 16 (z_hi: 2, z_lo: 8; z = z_hi * 8 + z_lo), core: 2. Of those that a mesh axis runs over, the one named last changes fastest.
Arguments:
- rhs: float32 [2, 50, 131072], P(None, None, ('wide', 'narrow')), may hold values from -6 to 6
- block_inv: float32 [50, 50, 131072], P(None, None, ('wide', 'narrow')), may hold values from -0.875 to 0.875
- line_order: int32 [512, 256], P(('wide', 'narrow')), may hold values from 0 to 255, each once within a row
- line_coef: float32 [2, 131072], P(None, ('wide', 'narrow')), may hold values from 0.2 to 1
- line_faces: float32 [2, 50, 50], replicated, may hold values from -0.875 to 0.875
- intersection: int32 [512, 4, 128], P(('wide', 'narrow')), may hold values from 0 to 255
- intersection_coef: float32 [512, 4, 128], P(('wide', 'narrow')), may hold values from 0.2 to 1
- ghost_face: float32 [50, 50], replicated, may hold values from -0.875 to 0.875
- modes: float32 [131072, 384], P(('wide', 'narrow')), may hold values from -0.3125 to 0.3125
- coarse_inv: float32 [384, 384], replicated, may hold values from -0.015625 to 0.015625
Outputs:
- precond: float32 [2, 50, 131072], P(None, None, ('wide', 'narrow'))
Inputs may be any that keep to these rules, and one draw needn't show every extreme that they name: Each row of line_order lists each of the 256 local elements once. `intersection`: entries are local element numbers of their own subdomain; an element may appear several times.
All inputs are finite; a program needn't handle non-finite values.
Results may differ from a plain program's by a relative error of at most 0.0003.
Values sent between devices are 32-bit elements; how exact they have to be, the bound alone decides.
No kernel may reach another device: no remote copies, remote signals or barrier semaphores. Data moves between devices by JAX's collectives and lax.ppermute only.
A program may use at most 64 MiB of HBM per device.

v0:
```python
import jax
import jax.numpy as jnp
from jax import lax
from jax.sharding import PartitionSpec as P

LINE = 32


def partner(block, axis, distance):
    count = lax.axis_size(axis)
    route = []
    for low in range(count):
        high = low | 1 << distance
        if high != low and high < count:
            route += [(low, high), (high, low)]
    return lax.ppermute(block, axis, route)


def colour_rows(vector, layers):
    return jnp.stack([jnp.take(vector, layers[colour], axis=1) for colour in range(4)])


def boosted_rhs(vector, weights, received, ghost_face, margin_hit):
    pushed = (
        jnp.einsum("ij,cjk->cik", ghost_face, received, precision=lax.Precision.HIGHEST)
        * weights[:, None, :]
    )
    columns = jnp.transpose(pushed, (1, 0, 2)).reshape(vector.shape[0], -1)
    return vector + jnp.dot(columns, margin_hit, precision=lax.Precision.HIGHEST)


def line_solve(vector, order_hit, blocks, coefs, line_faces):
    ordered = jnp.einsum("ie,pe->ip", vector, order_hit, precision=lax.Precision.HIGHEST)
    first = jnp.einsum("ijp,jp->ip", blocks, ordered, precision=lax.Precision.HIGHEST)
    spot = jnp.arange(ordered.shape[1]) % LINE
    before = jnp.where(spot[None, :] > 0, jnp.roll(first, 1, axis=1), 0.0)
    after = jnp.where(spot[None, :] < LINE - 1, jnp.roll(first, -1, axis=1), 0.0)
    coupled = ordered + coefs[0] * jnp.dot(line_faces[0], before, precision=lax.Precision.HIGHEST)
    coupled = coupled + coefs[1] * jnp.dot(line_faces[1], after, precision=lax.Precision.HIGHEST)
    second = jnp.einsum("ijp,jp->ip", blocks, coupled, precision=lax.Precision.HIGHEST)
    return jnp.dot(second, order_hit, precision=lax.Precision.HIGHEST)


def coarse_term(vector, modes):
    return jnp.dot(vector, modes, precision=lax.Precision.HIGHEST)


def shards(
    rhs,
    block_inv,
    line_order,
    line_coef,
    line_faces,
    intersection,
    intersection_coef,
    ghost_face,
    modes,
    coarse_inv,
):
    order = line_order[0]
    layers = intersection[0]
    weights = intersection_coef[0]
    count = rhs.shape[2]
    element_ids = jnp.arange(count, dtype=jnp.int32)
    margin_hit = (layers.reshape(-1)[:, None] == element_ids[None, :]).astype(jnp.float32)
    order_hit = (order[:, None] == element_ids[None, :]).astype(jnp.float32)
    sent = [colour_rows(rhs[app], layers) for app in range(2)]
    received = [
        jnp.stack([partner(sent[app][colour], "wide", colour) for colour in range(4)])
        for app in range(2)
    ]
    coarse = [lax.psum(coarse_term(rhs[app], modes), ("wide", "narrow")) for app in range(2)]
    results = []
    for app in range(2):
        lifted = boosted_rhs(rhs[app], weights, received[app], ghost_face, margin_hit)
        local = line_solve(lifted, order_hit, block_inv, line_coef, line_faces)
        solved = jnp.dot(coarse[app], coarse_inv, precision=lax.Precision.HIGHEST)
        results.append(local + jnp.dot(solved, modes.T, precision=lax.Precision.HIGHEST))
    return jnp.stack(results)


def solution(mesh):
    in_specs = (
        P(None, None, ("wide", "narrow")),
        P(None, None, ("wide", "narrow")),
        P(("wide", "narrow"), None),
        P(None, ("wide", "narrow")),
        P(),
        P(("wide", "narrow"), None, None),
        P(("wide", "narrow"), None, None),
        P(),
        P(("wide", "narrow"), None),
        P(),
    )
    out_specs = P(None, None, ("wide", "narrow"))
    return jax.shard_map(shards, mesh=mesh, in_specs=in_specs, out_specs=out_specs, check_vma=False)
```

profile of v0, /device:TPU:1, one launch (start us, length us, event | category | flops | bytes accessed | tf_op | source)
XLA Modules:
  0.0 533.2 jit_solution(1069415936034999061)
XLA Ops:
  6.5 1.4 compare_and_fusion.3
  8.0 1.1 fusion.68
  9.2 0.6 gather_fusion
  10.0 0.7 copy-done.2
  11.3 0.7 copy.31
  12.0 1.5 select_bitcast_fusion.7
  13.6 8.7 %collective-permute-start = (f32[50,128]{1,0:T(8,128)}, f32[50,128]{1,0:T(8,128)}, u32[]{:S(2)}, u32[]{:S(2)}) collective-permute-start(f32[50,128]{1,0:T(8,128)} %get-tuple-element.38), channel_id=1, source_target_pairs={{0,8},{8,0},{16,24},{24,16},{32,40},{40,32},{48,56},{56,48},{64,72... | collective-permute-start | bytes 76808 | tf_op jit(solution)/shard_map/ppermute | solution.py:16
  22.9 2.1 gather_fusion.1
  25.1 1.5 gather_fusion.5
  26.6 0.9 copy.24
  27.6 0.7 copy.32
  28.3 1.4 select_bitcast_fusion.6
  29.6 1.9 collective-permute-start.1
  31.5 0.7 pad_clamp_fusion.1
  32.2 2.1 gather_fusion.2
  34.4 1.5 gather_fusion.6
  35.9 0.9 copy.25
  36.8 0.7 copy.33
  37.5 1.4 select_bitcast_fusion.5
  38.9 1.9 collective-permute-start.2
  41.4 2.1 gather_fusion.3
  43.6 1.5 gather_fusion.7
  45.1 0.9 copy.26
  46.0 0.7 copy.34
  46.7 1.4 select_bitcast_fusion.4
  48.1 1.9 collective-permute-start.3
  50.0 2.3 collective-permute-start.4
  52.4 2.1 fusion.60
  54.5 2.1 fusion.62
  56.6 0.9 fusion.73
  57.6 0.8 fusion.74
  58.3 3.2 collective-permute-start.5
  61.6 5.8 %collective-permute-start.6 = (f32[50,128]{1,0:T(8,128)}, f32[50,128]{1,0:T(8,128)S(1)}, u32[]{:S(2)}, u32[]{:S(2)}) collective-permute-start(f32[50,128]{1,0:T(8,128)} %get-tuple-element.43), channel_id=1, source_target_pairs={{0,32},{32,0},{8,40},{40,8},{16,48},{48,16},{24,56},{56,24},{64,96... | collective-permute-start | bytes 76808 | tf_op jit(solution)/shard_map/ppermute | solution.py:16
  67.4 3.6 collective-permute-start.7
  71.0 1.1 fusion.1
  72.2 1.6 convolution_add_fusion.1
  73.8 1.0 fusion.15
  75.4 0.9 fusion
  76.4 0.7 convolution_add_fusion
  78.0 0.8 multiply_reduce_fusion.2
  79.5 0.9 multiply_reduce_fusion
  80.4 438.2 %all-reduce.3.cloned.1.call-done = (f32[50,384]{1,0:T(8,128)}, f32[50,384]{1,0:T(8,128)}) async-done(((f32[50,384]{1,0:T(8,128)}, f32[50,384]{1,0:T(8,128)}), (f32[50,384]{1,0:T(8,128)}, f32[50,384]{1,0:T(8,128)})) %all-reduce.3.cloned.1.call-update) | async-done | bytes 153616 | tf_op jit(solution)/shard_map/psum | solution.py:72
  518.6 1.3 fusion.75
  519.9 1.5 fusion.76
  521.4 1.3 fusion.77
  522.7 1.5 fusion.78
  524.5 1.1 fusion.2
  525.6 0.7 copy.36
  (52 shorter events, 4.7 us)
Async XLA Ops:
  6.5 512.1 %copy-start = (f32[384,384]{1,0:T(8,128)S(1)}, f32[384,384]{1,0:T(8,128)}, u32[]{:S(2)}) copy-start(f32[384,384]{1,0:T(8,128)} %param.21) | copy-start | bytes 1769476
  6.5 512.1 %all-reduce.3.cloned.1.call-start = ((), (), s32[]{:S(2)}) async-start(), calls=%async_computation | async-start | bytes 344064 | tf_op jit(solution)/shard_map/psum | solution.py:72
  9.2 0.7 copy-start.4
  9.8 62.4 %copy-start.6 = (s32[1,4,128]{2,1,0:T(4,128)S(1)}, s32[1,4,128]{2,1,0:T(4,128)}, u32[]{:S(2)}) copy-start(s32[1,4,128]{2,1,0:T(4,128)} %param.17) | copy-start | bytes 6148
  10.0 0.7 copy-start.2
  11.3 63.5 %copy-start.1 = (f32[50,50,256]{2,1,0:T(8,128)S(1)}, f32[50,50,256]{2,1,0:T(8,128)}, u32[]{:S(2)}) copy-start(f32[50,50,256]{2,1,0:T(8,128)} %param.13) | copy-start | bytes 7680004
  13.6 44.8 %collective-permute-start = (f32[50,128]{1,0:T(8,128)}, f32[50,128]{1,0:T(8,128)}, u32[]{:S(2)}, u32[]{:S(2)}) collective-permute-start(f32[50,128]{1,0:T(8,128)} %get-tuple-element.38), channel_id=1, source_target_pairs={{0,8},{8,0},{16,24},{24,16},{32,40},{40,32},{48,56},{56,48},{64,72... | collective-permute-start | bytes 76808 | tf_op jit(solution)/shard_map/ppermute | solution.py:16
  29.6 31.9 %collective-permute-start.1 = (f32[50,128]{1,0:T(8,128)}, f32[50,128]{1,0:T(8,128)}, u32[]{:S(2)}, u32[]{:S(2)}) collective-permute-start(f32[50,128]{1,0:T(8,128)} %get-tuple-element.40), channel_id=1, source_target_pairs={{0,16},{16,0},{8,24},{24,8},{32,48},{48,32},{40,56},{56,40},{64,80... | collective-permute-start | bytes 76808 | tf_op jit(solution)/shard_map/ppermute | solution.py:16
  38.9 28.4 %collective-permute-start.2 = (f32[50,128]{1,0:T(8,128)}, f32[50,128]{1,0:T(8,128)}, u32[]{:S(2)}, u32[]{:S(2)}) collective-permute-start(f32[50,128]{1,0:T(8,128)} %get-tuple-element.42), channel_id=1, source_target_pairs={{0,32},{32,0},{8,40},{40,8},{16,48},{48,16},{24,56},{56,24},{64,96... | collective-permute-start | bytes 76808 | tf_op jit(solution)/shard_map/ppermute | solution.py:16
  48.1 22.9 %collective-permute-start.3 = (f32[50,128]{1,0:T(8,128)}, f32[50,128]{1,0:T(8,128)}, u32[]{:S(2)}, u32[]{:S(2)}) collective-permute-start(f32[50,128]{1,0:T(8,128)} %get-tuple-element.44), channel_id=1, source_target_pairs={{0,64},{64,0},{8,72},{72,8},{16,80},{80,16},{24,88},{88,24},{32,96... | collective-permute-start | bytes 76808 | tf_op jit(solution)/shard_map/ppermute | solution.py:16
  50.0 25.3 %collective-permute-start.4 = (f32[50,128]{1,0:T(8,128)}, f32[50,128]{1,0:T(8,128)S(1)}, u32[]{:S(2)}, u32[]{:S(2)}) collective-permute-start(f32[50,128]{1,0:T(8,128)} %get-tuple-element.39), channel_id=1, source_target_pairs={{0,8},{8,0},{16,24},{24,16},{32,40},{40,32},{48,56},{56,48},{64,72... | collective-permute-start | bytes 76808 | tf_op jit(solution)/shard_map/ppermute | solution.py:16
  54.5 20.9 %copy-start.5 = (f32[50,50]{1,0:T(8,128)S(1)}, f32[50,50]{1,0:T(8,128)}, u32[]{:S(2)}) copy-start(f32[50,50]{1,0:T(8,128)} %param.19) | copy-start | bytes 30004
  58.3 17.0 %collective-permute-start.5 = (f32[50,128]{1,0:T(8,128)}, f32[50,128]{1,0:T(8,128)S(1)}, u32[]{:S(2)}, u32[]{:S(2)}) collective-permute-start(f32[50,128]{1,0:T(8,128)} %get-tuple-element.41), channel_id=1, source_target_pairs={{0,16},{16,0},{8,24},{24,8},{32,48},{48,32},{40,56},{56,40},{64,80... | collective-permute-start | bytes 76808 | tf_op jit(solution)/shard_map/ppermute | solution.py:16
  61.6 13.8 %collective-permute-start.6 = (f32[50,128]{1,0:T(8,128)}, f32[50,128]{1,0:T(8,128)S(1)}, u32[]{:S(2)}, u32[]{:S(2)}) collective-permute-start(f32[50,128]{1,0:T(8,128)} %get-tuple-element.43), channel_id=1, source_target_pairs={{0,32},{32,0},{8,40},{40,8},{16,48},{48,16},{24,56},{56,24},{64,96... | collective-permute-start | bytes 76808 | tf_op jit(solution)/shard_map/ppermute | solution.py:16
  67.4 8.0 %collective-permute-start.7 = (f32[50,128]{1,0:T(8,128)S(1)}, f32[50,128]{1,0:T(8,128)S(1)}, u32[]{:S(2)}, u32[]{:S(2)}) collective-permute-start(f32[50,128]{1,0:T(8,128)S(1)} %get-tuple-element.45), channel_id=1, source_target_pairs={{0,64},{64,0},{8,72},{72,8},{16,80},{80,16},{24,88},{88,24},{32,96... | collective-permute-start | bytes 76808 | tf_op jit(solution)/shard_map/ppermute | solution.py:16
  71.0 5.4 %copy-start.3 = (f32[1,50,256]{1,2,0:T(8,128)S(1)}, f32[1,50,256]{1,2,0:T(8,128)}, u32[]{:S(2)}) copy-start(f32[1,50,256]{1,2,0:T(8,128)} %copy-done.2) | copy-start | bytes 153604
  72.2 4.9 copy-start.7
Sparse Core Ops, SparseCore 0:
  56.7 461.8 all-reduce.2
where the time goes:
time: 534 us; the launch traced here: 533 us
  waiting for transfers between devices  438 us (82%)
  starting transfers between devices  29.4 us (6%)
  local copies, waits for them, and re-layouts  22.8 us (4%)
  matrix products  17.9 us (3%)
  between operations  13.8 us (3%)
  other arithmetic  11 us (2%)
    psum x1, waiting for transfers between devices, shards(): lax.psum(coarse_term(rhs[app], modes), ('wide', 'narrow'))  438 us
    ppermute x8, starting transfers between devices, partner(): return lax.ppermute(block, axis, route)  29.4 us
    gather x16, local copies, waits for them, and re-layouts, colour_rows(): jnp.take(vector, layers[colour], axis=1)  18 us
  transfers between devices with their start and end apart: 9, of which 1 were waited for; matrix products, arithmetic and copies ran while one was open for 7% of the time, Pallas kernels for 0%

commit v1 on v0

v1 whole, which is shorter than its diff:
```python
import jax
import jax.numpy as jnp
import numpy as np
from jax import lax
from jax.sharding import PartitionSpec as P

LINE = 32
ALL = ("wide", "narrow")
PLANE = 32
RING = 16
ROWS = 4
HI = lax.Precision.HIGHEST


def groups():
    place = np.arange(PLANE * RING).reshape(2, PLANE, 8)
    plane = place.transpose(0, 2, 1).reshape(-1, PLANE).tolist()
    ring = place.transpose(1, 0, 2).reshape(-1, RING).tolist()
    return plane, ring


def swap(blocks, groups_of):
    return lax.all_to_all(blocks, ALL, 0, 0, axis_index_groups=groups_of)


def flip(blocks, colour):
    half = 1 << colour
    shape = blocks.shape
    return blocks.reshape((-1, 2, half) + shape[1:])[:, ::-1].reshape(shape)


def shards(
    rhs,
    block_inv,
    line_order,
    line_coef,
    line_faces,
    intersection,
    intersection_coef,
    ghost_face,
    modes,
    coarse_inv,
):
    plane, ring = groups()
    order = line_order[0]
    layers = intersection[0].reshape(-1)
    weights = intersection_coef[0].reshape(-1)
    apps, ndof, count = rhs.shape
    kc = modes.shape[1]
    rows = apps * ndof
    ids = jnp.arange(count, dtype=jnp.int32)
    both = jnp.transpose(rhs, (1, 0, 2)).reshape(rows, count)
    pick = (ids[:, None] == layers[None, :]).astype(jnp.float32)
    front = jnp.dot(both, jnp.concatenate([modes, pick], axis=1), precision=HI)
    out0 = jnp.pad(front, ((0, PLANE * ROWS - rows), (0, 0))).reshape(PLANE, ROWS, -1)
    in0 = swap(out0, plane)
    part = jnp.sum(in0[:, :, :kc], axis=0)
    in1 = swap(jnp.broadcast_to(part, (RING, ROWS, kc)), ring)
    coarse = jnp.sum(in1, axis=0)
    span = intersection.shape[2]
    pieces = [flip(in0[:, :, kc + c * span : kc + (c + 1) * span], c) for c in range(4)]
    out2 = jnp.concatenate([jnp.broadcast_to(coarse, (PLANE, ROWS, kc))] + pieces, axis=2)
    in2 = swap(out2, plane).reshape(PLANE * ROWS, -1)[:rows]
    coarse_res = in2[:, :kc]
    received = in2[:, kc:]
    lift = jnp.dot(coarse_inv, modes.T, precision=HI)
    pushed = jnp.einsum("ij,jx->ix", ghost_face, received.reshape(ndof, -1), precision=HI).reshape(rows, -1)
    pushed = pushed * weights[None, :]
    hit = (ids[:, None] == order[None, :]).astype(jnp.float32)
    margin = (layers[:, None] == order[None, :]).astype(jnp.float32)
    ordered = jnp.dot(both, hit, precision=HI) + jnp.dot(pushed, margin, precision=HI)
    results = []
    spot = ids % LINE
    first_of = spot[None, :] > 0
    last_of = spot[None, :] < LINE - 1
    split = ordered.reshape(ndof, apps, count)
    for app in range(apps):
        mine = split[:, app]
        first = jnp.einsum("ijp,jp->ip", block_inv, mine, precision=HI)
        before = jnp.where(first_of, jnp.roll(first, 1, axis=1), 0.0)
        after = jnp.where(last_of, jnp.roll(first, -1, axis=1), 0.0)
        coupled = mine + line_coef[0] * jnp.dot(line_faces[0], before, precision=HI)
        coupled = coupled + line_coef[1] * jnp.dot(line_faces[1], after, precision=HI)
        results.append(jnp.einsum("ijp,jp->ip", block_inv, coupled, precision=HI))
    second = jnp.stack(results, axis=1).reshape(rows, count)
    total = jnp.dot(second, hit.T, precision=HI) + jnp.dot(coarse_res, lift, precision=HI)
    return jnp.transpose(total.reshape(ndof, apps, count), (1, 0, 2))


def solution(mesh):
    in_specs = (
        P(None, None, ALL),
        P(None, None, ALL),
        P(ALL, None),
        P(None, ALL),
        P(),
        P(ALL, None, None),
        P(ALL, None, None),
        P(),
        P(ALL, None),
        P(),
    )
    out_specs = P(None, None, ALL)
    return jax.shard_map(shards, mesh=mesh, in_specs=in_specs, out_specs=out_specs, check_vma=False)
```

time: 534 us -> 95.2 us (0.18)
  waiting for transfers between devices: 438 us -> 29.8 us
  between operations: 13.8 us -> 0.3 us
  other arithmetic: 11 us -> 3.43 us
  matrix products: 17.9 us -> 12.3 us
    psum x1 -> x0, waiting for transfers between devices: 438 us -> none  [shards(): lax.psum(coarse_term(rhs[app], modes), ('wide', 'narrow'))]
    all_to_all x0 -> x3, starting transfers between devices: none -> 30.2 us  [swap(): return lax.all_to_all(blocks, ALL, 0, 0, axis_index_groups=groups_of)]
    all_to_all x0 -> x3, waiting for transfers between devices: none -> 29.8 us  [swap(): return lax.all_to_all(blocks, ALL, 0, 0, axis_index_groups=groups_of)]
    ppermute x8 -> x0, starting transfers between devices: 29.4 us -> none  [partner(): return lax.ppermute(block, axis, route)]
    gather x16 -> x0, local copies, waits for them, and re-layouts: 18 us -> none  [colour_rows(): jnp.take(vector, layers[colour], axis=1)]
    reshape x0 -> x7, local copies, waits for them, and re-layouts: none -> 7.57 us  [the longest x1 1.69 us: shards(): received.reshape(ndof, -1)]
    select_n x4 -> x0, other arithmetic: 5.63 us -> none  [colour_rows(): jnp.take(vector, layers[colour], axis=1)]
    dot_general x18 -> x11, matrix products: 17.9 us -> 12.3 us  [the longest x1 2.68 us: shards(): lift = jnp.dot(coarse_inv, modes.T, precision=HI)]
  transfers between devices with their start and end apart: 9 -> 3, of which waited for: 1 -> 3; matrix products, arithmetic and copies ran while one was open for 7% -> 4% of each run, Pallas kernels for 0% -> 0%
where the time goes in v1:
time: 95.2 us; the launch traced here: 94.5 us
  starting transfers between devices  30.2 us (32%)
  waiting for transfers between devices  29.8 us (31%)
  local copies, waits for them, and re-layouts  18.4 us (19%)
  matrix products  12.3 us (13%)
  other arithmetic  3.43 us (4%)
    all_to_all x3, starting transfers between devices, swap(): return lax.all_to_all(blocks, ALL, 0, 0, axis_index_groups=groups_of)  30.2 us
    all_to_all x3, waiting for transfers between devices, swap(): return lax.all_to_all(blocks, ALL, 0, 0, axis_index_groups=groups_of)  29.8 us
    slice x2, local copies, waits for them, and re-layouts, shards(): in2 = swap(out2, plane).reshape(PLANE * ROWS, -1)[:rows]  3.59 us
    unnamed x23, local copies, waits for them, and re-layouts  2.71 us
    dot_general x1, matrix products, shards(): lift = jnp.dot(coarse_inv, modes.T, precision=HI)  2.68 us
    dot_general x1, matrix products, shards(): jnp.einsum('ij,jx->ix', ghost_face, received.reshape(ndof, -1), precision...  1.96 us
  transfers between devices with their start and end apart: 3, of which 3 were waited for; matrix products, arithmetic and copies ran while one was open for 4% of the time, Pallas kernels for 0%

profile of v1, /device:TPU:1, one launch (start us, length us, event | category | flops | bytes accessed | tf_op | source)
XLA Modules:
  0.0 94.5 jit_solution(12115151101229794146)
XLA Ops:
  0.0 0.8 fusion.14
  0.8 1.0 %reshape.65 = f32[100,256]{1,0:T(8,128)S(1)} reshape(f32[50,2,256]{2,1,0:T(2,128)} %bitcast.101) | data formatting | bytes 204800 | tf_op jit(solution)/shard_map/reshape | solution.py:52
  1.8 1.7 %convolution_bitcast_fusion = f32[100,896]{1,0:T(8,128)S(1)} fusion(f32[100,256]{1,0:T(8,128)S(1)} %reshape.65, f32[256,512]{1,0:T(8,128)S(1)} %fusion.14, f32[256,384]{1,0:T(8,128)} %param.18), kind=kOutput, calls=%fused_computation.4 | convolution fusion | flops 275480576 | bytes 1378304 | tf_op jit(solution)/shard_map/dot_general | solution.py:54
  3.5 0.0 copy-start.8
  3.6 0.9 reshape.66
  4.5 10.4 %all-to-all-start = ((f32[32,4,896]{2,1,0:T(4,128)}), f32[32,4,896]{2,1,0:T(4,128)S(1)}, u32[]{:S(2)}, u32[]{:S(2)}) async-start(f32[32,4,896]{2,1,0:T(4,128)} %reshape.66), calls=%async_computation | async-start | bytes 917504 | tf_op jit(solution)/shard_map/all_to_all | solution.py:23
  14.9 10.8 %all-to-all-done = f32[32,4,896]{2,1,0:T(4,128)S(1)} async-done(((f32[32,4,896]{2,1,0:T(4,128)}), f32[32,4,896]{2,1,0:T(4,128)S(1)}, u32[]{:S(2)}, u32[]{:S(2)}) %all-to-all-start) | async-done | bytes 458784 | tf_op jit(solution)/shard_map/all_to_all | solution.py:23
  25.8 0.7 broadcast_in_dim.40
  26.4 13.0 %all-to-all-start.1 = ((f32[16,4,384]{2,1,0:T(4,128)}), f32[16,4,384]{2,1,0:T(4,128)S(1)}, u32[]{:S(2)}, u32[]{:S(2)}) async-start(f32[16,4,384]{2,1,0:T(4,128)} %broadcast_in_dim.40), calls=%async_computation.1 | async-start | bytes 196608 | tf_op jit(solution)/shard_map/all_to_all | solution.py:23
  39.5 0.5 broadcast_compare_fusion
  40.0 0.5 broadcast_compare_fusion.1
  40.6 0.0 copy-start.4
  40.6 10.7 %all-to-all-done.1 = f32[16,4,384]{2,1,0:T(4,128)S(1)} async-done(((f32[16,4,384]{2,1,0:T(4,128)}), f32[16,4,384]{2,1,0:T(4,128)S(1)}, u32[]{:S(2)}, u32[]{:S(2)}) %all-to-all-start.1) | async-done | bytes 98336 | tf_op jit(solution)/shard_map/all_to_all | solution.py:23
  51.4 0.7 broadcast_dynamic-update-slice_fusion
  52.1 0.7 constant_dynamic-update-slice_fusion.3
  52.8 0.6 constant_dynamic-update-slice_fusion.2
  53.4 0.6 constant_dynamic-update-slice_fusion.1
  54.0 0.7 constant_dynamic-update-slice_fusion
  54.7 6.9 %all-to-all-start.2 = ((f32[32,4,896]{2,1,0:T(4,128)}), f32[32,4,896]{2,1,0:T(4,128)}, u32[]{:S(2)}, u32[]{:S(2)}) async-start(f32[32,4,896]{2,1,0:T(4,128)} %constant_dynamic-update-slice_fusion), calls=%async_computation.2 | async-start | bytes 917504 | tf_op jit(solution)/shard_map/all_to_all | solution.py:23
  61.6 0.0 copy-start.1
  61.6 2.7 %fusion.58 = f32[384,256]{1,0:T(8,128)} fusion(f32[384,384]{1,0:T(8,128)S(1)} %copy-done, f32[256,384]{1,0:T(8,128)} %param.18), kind=kOutput, calls=%fused_computation.90 | convolution fusion | flops 452984832 | bytes 1376256 | tf_op jit(solution)/shard_map/dot_general | solution.py:66
  64.3 8.2 %all-to-all-done.2 = f32[32,4,896]{2,1,0:T(4,128)} async-done(((f32[32,4,896]{2,1,0:T(4,128)}), f32[32,4,896]{2,1,0:T(4,128)}, u32[]{:S(2)}, u32[]{:S(2)}) %all-to-all-start.2) | async-done | bytes 458784 | tf_op jit(solution)/shard_map/all_to_all | solution.py:23
  72.5 1.7 %slice.105 = f32[25,4,896]{2,1,0:T(4,128)} slice(f32[32,4,896]{2,1,0:T(4,128)} %all-to-all-done.2), slice={[0:25], [0:4], [0:896]} | slice | bytes 716800 | tf_op jit(solution)/shard_map/slice | solution.py:63
  74.3 1.9 %slice.83 = f32[100,896]{1,0:T(8,128)} reshape(f32[25,4,896]{2,1,0:T(4,128)} %slice.105) | data formatting | bytes 716800 | tf_op jit(solution)/shard_map/slice | solution.py:63
  76.1 1.6 %slice.106 = f32[100,512]{1,0:T(8,128)} slice(f32[100,896]{1,0:T(8,128)} %slice.83), slice={[0:100], [384:896]} | slice | bytes 409600 | tf_op jit(solution)/shard_map/slice | solution.py:65
  77.8 1.7 %reshape.75 = f32[50,1024]{1,0:T(8,128)} reshape(f32[100,512]{1,0:T(8,128)} %slice.106) | data formatting | bytes 409600 | tf_op jit(solution)/shard_map/reshape | solution.py:67
  79.4 2.0 %convolution_bitcast_fusion.1 = f32[50,1024]{1,0:T(8,128)} fusion(f32[50,1024]{1,0:T(8,128)} %reshape.75, f32[50,50]{1,0:T(8,128)S(1)} %copy-done.4), kind=kOutput, calls=%fused_computation.5 | convolution fusion | flops 30720000 | bytes 419600 | tf_op jit(solution)/shard_map/ij,jx->ix/dot_general | solution.py:67
  81.4 1.7 %reshape.76 = f32[100,512]{1,0:T(8,128)} reshape(f32[50,1024]{1,0:T(8,128)} %convolution_bitcast_fusion.1) | data formatting | bytes 409600 | tf_op jit(solution)/shard_map/reshape | solution.py:67
  83.1 1.3 %fusion.15 = f32[100,256]{1,0:T(8,128)S(1)} fusion(s32[256]{0:T(256)S(1)} %bitcast.102, s32[512]{0:T(512)} %bitcast.110, f32[100,512]{1,0:T(8,128)} %reshape.76, f32[512]{0:T(512)} %bitcast.111), kind=kOutput, calls=%fused_computation.28 | convolution fusion | flops 157468672 | bytes 312320 | tf_op jit(solution)/shard_map/dot_general | solution.py:71
  84.4 1.8 %fusion = f32[100,256]{1,0:T(8,128)} fusion(f32[100,256]{1,0:T(8,128)S(1)} %fusion.15, f32[100,256]{1,0:T(8,128)} %copy-done.2, s32[256]{0:T(256)S(1)} %bitcast.103), kind=kOutput, calls=%fused_computation.8 | convolution fusion | flops 78734336 | bytes 308224 | tf_op jit(solution)/shard_map/dot_general | solution.py:71
  86.2 1.6 %reshape.77 = f32[50,2,256]{2,1,0:T(2,128)} reshape(f32[100,256]{1,0:T(8,128)} %fusion) | data formatting | bytes 204800 | tf_op jit(solution)/shard_map/reshape | solution.py:76
  87.8 1.1 %fusion.51 = (f32[50,1,256]{2,1,0:T(1,128)S(1)}, f32[50,1,256]{2,1,0:T(1,128)S(1)}) fusion(f32[50,2,256]{2,1,0:T(2,128)} %reshape.77), kind=kLoop, calls=%fused_computation.83 | loop fusion | bytes 204800 | tf_op jit(solution)/shard_map/slice | solution.py:78
  88.9 0.3 multiply_reduce_fusion.3
  89.2 0.1 fusion.54
  89.2 0.1 fusion.55
  89.3 0.3 fusion.10
  89.6 0.3 fusion.8
  89.9 0.8 multiply_reduce_fusion.2
  90.7 0.1 fusion.52
  90.8 0.1 fusion.53
  90.8 0.3 fusion.5
  91.1 0.3 fusion.3
  91.4 0.3 multiply_reduce_fusion
  91.8 0.1 pad_maximum_fusion
  91.9 0.1 reshape.78
  92.0 1.5 %fusion.20 = f32[100,256]{1,0:T(8,128)S(1)} fusion(f32[384,256]{1,0:T(8,128)} %fusion.58, f32[100,896]{1,0:T(8,128)} %slice.83), kind=kOutput, calls=%fused_computation.35 | convolution fusion | flops 117964800 | bytes 655360 | tf_op jit(solution)/shard_map/dot_general | solution.py:86
  93.5 0.3 convolution_add_fusion
  93.8 0.7 reshape.79
  (28 shorter events, 0.3 us)
Async XLA Ops:
  0.0 61.6 %copy-start = (f32[384,384]{1,0:T(8,128)S(1)}, f32[384,384]{1,0:T(8,128)}, u32[]{:S(2)}) copy-start(f32[384,384]{1,0:T(8,128)} %param.19) | copy-start | bytes 1769476
  0.0 14.8 %copy-start.3 = (f32[2,50,50]{2,0,1:T(2,128)S(1)}, f32[2,50,50]{2,0,1:T(2,128)}, u32[]{:S(2)}) copy-start(f32[2,50,50]{2,0,1:T(2,128)} %param.14) | copy-start | bytes 60004
  1.8 38.8 %copy-start.2 = (f32[100,256]{1,0:T(8,128)}, f32[100,256]{1,0:T(8,128)S(1)}, u32[]{:S(2)}) copy-start(f32[100,256]{1,0:T(8,128)S(1)} %reshape.65) | copy-start | bytes 307204
  3.5 58.1 %copy-start.8 = (f32[2,256]{1,0:T(2,128)S(1)}, f32[2,256]{1,0:T(2,128)}, u32[]{:S(2)}) copy-start(f32[2,256]{1,0:T(2,128)} %param.13) | copy-start | bytes 6148
  4.5 21.3 %all-to-all-start = ((f32[32,4,896]{2,1,0:T(4,128)}), f32[32,4,896]{2,1,0:T(4,128)S(1)}, u32[]{:S(2)}, u32[]{:S(2)}) async-start(f32[32,4,896]{2,1,0:T(4,128)} %reshape.66), calls=%async_computation | async-start | bytes 917504 | tf_op jit(solution)/shard_map/all_to_all | solution.py:23
  26.4 24.9 %all-to-all-start.1 = ((f32[16,4,384]{2,1,0:T(4,128)}), f32[16,4,384]{2,1,0:T(4,128)S(1)}, u32[]{:S(2)}, u32[]{:S(2)}) async-start(f32[16,4,384]{2,1,0:T(4,128)} %broadcast_in_dim.40), calls=%async_computation.1 | async-start | bytes 196608 | tf_op jit(solution)/shard_map/all_to_all | solution.py:23
  40.6 38.9 %copy-start.4 = (f32[50,50]{1,0:T(8,128)S(1)}, f32[50,50]{1,0:T(8,128)}, u32[]{:S(2)}) copy-start(f32[50,50]{1,0:T(8,128)} %param.17) | copy-start | bytes 30004
  54.0 29.0 %copy-start.5 = (s32[1,256]{1,0:T(1,128)S(1)}, s32[1,256]{1,0:T(1,128)}, u32[]{:S(2)}) copy-start(s32[1,256]{1,0:T(1,128)} %param.12) | copy-start | bytes 3076
  54.7 17.8 %all-to-all-start.2 = ((f32[32,4,896]{2,1,0:T(4,128)}), f32[32,4,896]{2,1,0:T(4,128)}, u32[]{:S(2)}, u32[]{:S(2)}) async-start(f32[32,4,896]{2,1,0:T(4,128)} %constant_dynamic-update-slice_fusion), calls=%async_computation.2 | async-start | bytes 917504 | tf_op jit(solution)/shard_map/all_to_all | solution.py:23
  61.6 27.2 %copy-start.1 = (f32[50,50,256]{2,1,0:T(8,128)S(1)}, f32[50,50,256]{2,1,0:T(8,128)}, u32[]{:S(2)}) copy-start(f32[50,50,256]{2,1,0:T(8,128)} %param.11) | copy-start | bytes 7680004
  81.4 7.9 %copy-start.7 = (pred[256]{0:T(512)(128)(4,1)S(1)}, pred[256]{0:T(512)(128)(4,1)}, u32[]{:S(2)}) copy-start(pred[256]{0:T(512)(128)(4,1)} %broadcast_compare_fusion) | copy-start | bytes 772
  81.4 8.2 %copy-start.6 = (pred[256]{0:T(512)(128)(4,1)S(1)}, pred[256]{0:T(512)(128)(4,1)}, u32[]{:S(2)}) copy-start(pred[256]{0:T(512)(128)(4,1)} %broadcast_compare_fusion.1) | copy-start | bytes 772

commit v2 on v1

v2 whole, which is shorter than its diff:
```python
import jax
import jax.numpy as jnp
import numpy as np
from jax import lax
from jax.experimental import pallas as pl
from jax.experimental.pallas import tpu as pltpu
from jax.sharding import PartitionSpec as P

LINE = 32
ALL = ("wide", "narrow")
PLANE = 32
RING = 16
ROWS = 4
PAD = 56
BLOCKS = 2 * PAD // ROWS
HI = lax.Precision.HIGHEST
F32 = jnp.float32
BF16 = jnp.bfloat16
VMEM = pl.BlockSpec(memory_space=pltpu.VMEM)


def groups():
    place = np.arange(PLANE * RING).reshape(2, PLANE, 8)
    plane = place.transpose(0, 2, 1).reshape(-1, PLANE).tolist()
    ring = place.transpose(1, 0, 2).reshape(-1, RING).tolist()
    return plane, ring


def swap(blocks, groups_of):
    return lax.all_to_all(blocks, ALL, 0, 0, axis_index_groups=groups_of)


def flip(blocks, colour):
    half = 1 << colour
    shape = blocks.shape
    return blocks.reshape((-1, 2, half) + shape[1:])[:, ::-1].reshape(shape)


def halves(x):
    high = x.astype(BF16)
    return high, (x - high.astype(F32)).astype(BF16)


def mul(a, b):
    return jnp.dot(a, b, preferred_element_type=F32)


def product(a, b):
    ah, al = halves(a)
    bh, bl = halves(b)
    n = a.shape[0]
    both = mul(jnp.concatenate([ah, al], axis=0), bh)
    return both[:n] + both[n:] + mul(ah, bl)


def choose(a, hit):
    ah, al = halves(a)
    n = a.shape[0]
    both = mul(jnp.concatenate([ah, al], axis=0), hit)
    return both[:n] + both[n:]


def one_hot(flags):
    return jnp.where(flags, 1.0, 0.0).astype(BF16)


def load_rows(x_ref, stack):
    ndof = x_ref.shape[0]
    stack[...] = jnp.zeros_like(stack)
    for app in range(2):
        stack[PAD * app : PAD * app + ndof, :] = x_ref[:, app, :]
    return stack[...]


def front_kernel(x_ref, modes_ref, layers_ref, out_ref, stack, wide):
    x = load_rows(x_ref, stack)
    count = x.shape[1]
    kc = modes_ref.shape[1]
    span = layers_ref.shape[1]
    wide[:, :kc] = product(x, modes_ref[...])
    ids = lax.broadcasted_iota(jnp.int32, (count, span), 0)
    for c in range(4):
        wide[:, kc + c * span : kc + (c + 1) * span] = choose(x, one_hot(ids == layers_ref[c : c + 1, :]))
    for k in range(BLOCKS):
        out_ref[k] = wide[ROWS * k : ROWS * k + ROWS, :]
    for k in range(BLOCKS, PLANE):
        out_ref[k] = jnp.zeros(out_ref.shape[1:], F32)


def front(x3, modes, layers):
    width = modes.shape[1] + layers.size
    return pl.pallas_call(
        front_kernel,
        out_shape=jax.ShapeDtypeStruct((PLANE, ROWS, width), F32),
        in_specs=[VMEM] * 3,
        scratch_shapes=[pltpu.VMEM((2 * PAD, x3.shape[2]), F32), pltpu.VMEM((2 * PAD, width), F32)],
        name="front",
    )(x3, modes, layers)


def solve(blocks_ref, x):
    ndof, _, count = blocks_ref.shape
    rows = []
    for i in range(ndof):
        block = blocks_ref[i]
        left = jnp.sum(block * x[:, :count], axis=0, keepdims=True)
        right = jnp.sum(block * x[:, count:], axis=0, keepdims=True)
        rows.append(jnp.concatenate([left, right], axis=1))
    return jnp.concatenate(rows, axis=0)


def tail_kernel(
    in_ref, x_ref, blocks_ref, order_ref, coef_ref, faces_ref, layers_ref, weights_ref, ghost_ref, lift_ref,
    out_ref, stack, wide,
):
    ndof, _, count = x_ref.shape
    kc = lift_ref.shape[0]
    x = load_rows(x_ref, stack)
    for k in range(BLOCKS):
        wide[ROWS * k : ROWS * k + ROWS, :] = in_ref[k]
    span = layers_ref.shape[0]
    received = jnp.concatenate([wide[PAD * a : PAD * a + ndof, kc:] for a in range(2)], axis=1)
    pushed = product(ghost_ref[...], received)
    weights = weights_ref[...]
    zero = jnp.zeros((PAD - ndof, span), F32)
    pushed = jnp.concatenate(
        [pushed[:, :span] * weights, zero, pushed[:, span:] * weights, zero], axis=0
    )
    order = order_ref[...]
    hit = one_hot(lax.broadcasted_iota(jnp.int32, (count, count), 0) == order)
    margin = one_hot(layers_ref[...] == order)
    ordered = choose(x, hit) + choose(pushed, margin)
    ordered = jnp.concatenate([ordered[:ndof], ordered[PAD : PAD + ndof]], axis=1)
    first = solve(blocks_ref, ordered)
    spot = lax.broadcasted_iota(jnp.int32, (1, count), 1) % LINE
    before = jnp.where(spot > 0, coef_ref[0:1, :], 0.0)
    after = jnp.where(spot < LINE - 1, coef_ref[1:2, :], 0.0)
    ahead = product(faces_ref[0], first)
    behind = product(faces_ref[1], first)
    coupled = []
    for a in range(2):
        cut = slice(a * count, a * count + count)
        coupled.append(
            ordered[:, cut]
            + before * pltpu.roll(ahead[:, cut], 1, 1)
            + after * pltpu.roll(behind[:, cut], count - 1, 1)
        )
    second = solve(blocks_ref, jnp.concatenate(coupled, axis=1))
    hole = jnp.zeros((PAD - ndof, count), F32)
    second = jnp.concatenate([second[:, :count], hole, second[:, count:], hole], axis=0)
    back = one_hot(lax.broadcasted_iota(jnp.int32, (count, count), 0) == order)
    sh, sl = halves(second)
    turned = lax.dot_general(
        jnp.concatenate([sh, sl], axis=0), back, (((1,), (1,)), ((), ())), preferred_element_type=F32
    )
    total = turned[: 2 * PAD] + turned[2 * PAD :] + product(wide[:, :kc], lift_ref[...])
    for a in range(2):
        out_ref[:, a, :] = total[PAD * a : PAD * a + ndof]


def tail(in2, x3, blocks, order, coef, faces, layers, weights, ghost, lift):
    ndof, apps, count = x3.shape
    return pl.pallas_call(
        tail_kernel,
        out_shape=jax.ShapeDtypeStruct(x3.shape, F32),
        in_specs=[VMEM] * 10,
        scratch_shapes=[pltpu.VMEM((2 * PAD, count), F32), pltpu.VMEM((2 * PAD, in2.shape[2]), F32)],
        name="tail",
    )(in2, x3, blocks, order, coef, faces, layers, weights, ghost, lift)


def shards(
    rhs,
    block_inv,
    line_order,
    line_coef,
    line_faces,
    intersection,
    intersection_coef,
    ghost_face,
    modes,
    coarse_inv,
):
    plane, ring = groups()
    kc = modes.shape[1]
    span = intersection.shape[2]
    x3 = jnp.transpose(rhs, (1, 0, 2))
    in0 = swap(front(x3, modes, intersection[0]), plane)
    part = jnp.sum(in0[:, :, :kc], axis=0)
    in1 = swap(jnp.broadcast_to(part, (RING, ROWS, kc)), ring)
    pieces = [flip(in0[:, :, kc + c * span : kc + (c + 1) * span], c) for c in range(4)]
    base = jnp.concatenate([jnp.zeros((PLANE, ROWS, kc), F32)] + pieces, axis=2)
    coarse = jnp.sum(in1, axis=0)
    out2 = lax.dynamic_update_slice(base, jnp.broadcast_to(coarse, (PLANE, ROWS, kc)), (0, 0, 0))
    in2 = swap(out2, plane)
    lift = jnp.dot(coarse_inv, modes.T, precision=HI)
    out = tail(
        in2,
        x3,
        block_inv,
        line_order,
        line_coef,
        line_faces,
        intersection.reshape(-1, 1),
        intersection_coef.reshape(1, -1),
        ghost_face,
        lift,
    )
    return jnp.transpose(out, (1, 0, 2))


def solution(mesh):
    in_specs = (
        P(None, None, ALL),
        P(None, None, ALL),
        P(ALL, None),
        P(None, ALL),
        P(),
        P(ALL, None, None),
        P(ALL, None, None),
        P(),
        P(ALL, None),
        P(),
    )
    out_specs = P(None, None, ALL)
    return jax.shard_map(shards, mesh=mesh, in_specs=in_specs, out_specs=out_specs, check_vma=False)
```

time: 95.2 us -> 73.4 us (0.77)
  local copies, waits for them, and re-layouts: 18.4 us -> 7.05 us
  matrix products: 12.3 us -> 1.53 us
  Pallas kernels: 0 us -> 7.33 us
  other arithmetic: 3.43 us -> 0.08 us
  waiting for transfers between devices: 29.8 us -> 27.3 us
    dot_general x10 -> x0, matrix products: 9.62 us -> none  [the longest x1 1.96 us: shards(): jnp.einsum('ij,jx->ix', ghost_face, received.reshape(ndof, -1), precision...]
    pallas_call x0 -> x2, Pallas kernels: none -> 7.33 us  [the longest x1 5.04 us: tail(): pl.pallas_call(tail_kernel, out_shape=jax.ShapeDtypeStruct(x3.shape, F32)...]
    reshape x7 -> x1, local copies, waits for them, and re-layouts: 7.57 us -> 0.85 us  [shards(): intersection.reshape(-1, 1)]
    slice x10 -> x0, local copies, waits for them, and re-layouts: 6.63 us -> none  [the longest x2 3.59 us: shards(): in2 = swap(out2, plane).reshape(PLANE * ROWS, -1)[:rows]]
    all_to_all x3, waiting for transfers between devices: 29.8 us -> 27.3 us  [swap(): return lax.all_to_all(blocks, ALL, 0, 0, axis_index_groups=groups_of)]
    dot_general x3 -> x0, other arithmetic: 1.39 us -> none  [the longest x2 1.09 us: shards(): results.append(jnp.einsum('ijp,jp->ip', block_inv, coupled, precision=HI))]
    unnamed x23 -> x15, local copies, waits for them, and re-layouts: 2.71 us -> 4.08 us
    dot_general x1, matrix products: 2.68 us -> 1.53 us  [shards(): lift = jnp.dot(coarse_inv, modes.T, precision=HI)]
  transfers between devices with their start and end apart: 3 -> 3, of which waited for: 3 -> 3; matrix products, arithmetic and copies ran while one was open for 4% -> 9% of each run, Pallas kernels for 0% -> 0%
where the time goes in v2:
time: 73.4 us; the launch traced here: 73 us
  starting transfers between devices  29.6 us (40%)
  waiting for transfers between devices  27.3 us (37%)
  Pallas kernels  7.33 us (10%)
  local copies, waits for them, and re-layouts  7.05 us (10%)
  matrix products  1.53 us (2%)
    all_to_all x3, starting transfers between devices, swap(): return lax.all_to_all(blocks, ALL, 0, 0, axis_index_groups=groups_of)  29.6 us
    all_to_all x3, waiting for transfers between devices, swap(): return lax.all_to_all(blocks, ALL, 0, 0, axis_index_groups=groups_of)  27.3 us
    pallas_call x1, Pallas kernels, tail(): pl.pallas_call(tail_kernel, out_shape=jax.ShapeDtypeStruct(x3.shape, F32)...  5.04 us
    unnamed x15, local copies, waits for them, and re-layouts  4.08 us
    pallas_call x1, Pallas kernels, front(): pl.pallas_call(front_kernel, out_shape=jax.ShapeDtypeStruct((PLANE, ROWS,...  2.3 us
    dot_general x1, matrix products, shards(): lift = jnp.dot(coarse_inv, modes.T, precision=HI)  1.53 us
  transfers between devices with their start and end apart: 3, of which 3 were waited for; matrix products, arithmetic and copies ran while one was open for 9% of the time, Pallas kernels for 0%

profile of v2, /device:TPU:1, one launch (start us, length us, event | category | flops | bytes accessed | tf_op | source)
XLA Modules:
  0.0 73.0 jit_solution(1304756098807127813)
XLA Ops:
  0.0 0.0 copy-start
  0.0 0.0 copy-start.4
  0.0 0.0 copy-start.3
  0.0 0.0 copy-start.2
  0.0 2.3 %front.1 = f32[32,4,896]{2,1,0:T(4,128)} custom-call(f32[50,2,256]{2,1,0:T(2,128)} %bitcast.15, f32[256,384]{1,0:T(8,128)} %modes_ref.1, s32[4,128]{1,0:T(4,128)} %bitcast.25), custom_call_target="tpu_custom_call" | custom-call | tf_op jit(solution)/shard_map/front/pallas_call | solution.py:92
  2.3 10.4 %all-to-all-start = ((f32[32,4,896]{2,1,0:T(4,128)}), f32[32,4,896]{2,1,0:T(4,128)S(1)}, u32[]{:S(2)}, u32[]{:S(2)}) async-start(f32[32,4,896]{2,1,0:T(4,128)} %front.1), calls=%async_computation | async-start | bytes 917504 | tf_op jit(solution)/shard_map/all_to_all | solution.py:30
  12.7 0.7 %broadcast_dynamic-update-slice_fusion.1 = f32[32,4,896]{2,1,0:T(4,128)} fusion(), kind=kLoop, calls=%fused_computation.2 | loop fusion | bytes 196608
  13.4 10.1 %all-to-all-done = f32[32,4,896]{2,1,0:T(4,128)S(1)} async-done(((f32[32,4,896]{2,1,0:T(4,128)}), f32[32,4,896]{2,1,0:T(4,128)S(1)}, u32[]{:S(2)}, u32[]{:S(2)}) %all-to-all-start) | async-done | bytes 458784 | tf_op jit(solution)/shard_map/all_to_all | solution.py:30
  23.7 0.7 broadcast_in_dim.10
  24.4 13.0 %all-to-all-start.1 = ((f32[16,4,384]{2,1,0:T(4,128)}), f32[16,4,384]{2,1,0:T(4,128)S(1)}, u32[]{:S(2)}, u32[]{:S(2)}) async-start(f32[16,4,384]{2,1,0:T(4,128)} %broadcast_in_dim.10), calls=%async_computation.1 | async-start | bytes 196608 | tf_op jit(solution)/shard_map/all_to_all | solution.py:30
  37.4 0.6 constant_dynamic-update-slice_fusion.3
  38.0 0.6 constant_dynamic-update-slice_fusion.2
  38.7 0.6 constant_dynamic-update-slice_fusion.1
  39.3 0.6 constant_dynamic-update-slice_fusion
  40.0 9.3 %all-to-all-done.1 = f32[16,4,384]{2,1,0:T(4,128)S(1)} async-done(((f32[16,4,384]{2,1,0:T(4,128)}), f32[16,4,384]{2,1,0:T(4,128)S(1)}, u32[]{:S(2)}, u32[]{:S(2)}) %all-to-all-start.1) | async-done | bytes 98336 | tf_op jit(solution)/shard_map/all_to_all | solution.py:30
  49.3 0.7 %broadcast_dynamic-update-slice_fusion = f32[32,4,896]{2,1,0:T(4,128)} fusion(f32[32,4,896]{2,1,0:T(4,128)} %constant_dynamic-update-slice_fusion, f32[4,384]{1,0:T(4,128)S(1)} %reduce_sum.19), kind=kLoop, calls=%fused_computation.1 | loop fusion | bytes 202752 | tf_op jit(solution)/shard_map/dynamic_update_slice | solution.py:194
  50.1 6.2 %all-to-all-start.2 = ((f32[32,4,896]{2,1,0:T(4,128)}), f32[32,4,896]{2,1,0:T(4,128)S(1)}, u32[]{:S(2)}, u32[]{:S(2)}) async-start(f32[32,4,896]{2,1,0:T(4,128)} %broadcast_dynamic-update-slice_fusion), calls=%async_computation.2 | async-start | bytes 917504 | tf_op jit(solution)/shard_map/all_to_all | solution.py:30
  56.3 0.0 copy-done.4
  56.3 0.9 %copy.18.layers_ref = s32[512,1]{1,0:T(8,128)} copy(s32[512,1]{0,1:T(1,128)S(1)} %bitcast.26) | data formatting | bytes 4096 | tf_op jit(solution)/shard_map/reshape | solution.py:204
  57.1 0.0 copy-done.3
  57.1 0.6 copy.17.faces_ref
  57.8 0.0 copy-done
  57.8 0.0 copy-done.2
  57.8 1.5 %fusion.1.lift_ref = f32[384,256]{1,0:T(8,128)} fusion(f32[384,384]{1,0:T(8,128)S(1)} %copy-done, f32[256,384]{1,0:T(8,128)S(1)} %copy-done.2), kind=kOutput, calls=%fused_computation.8 | convolution fusion | flops 452984832 | bytes 1376256 | tf_op jit(solution)/shard_map/dot_general | solution.py:196
  59.3 7.9 %all-to-all-done.2.in_ref = f32[32,4,896]{2,1,0:T(4,128)S(1)} async-done(((f32[32,4,896]{2,1,0:T(4,128)}), f32[32,4,896]{2,1,0:T(4,128)S(1)}, u32[]{:S(2)}, u32[]{:S(2)}) %all-to-all-start.2) | async-done | bytes 458784 | tf_op jit(solution)/shard_map/all_to_all | solution.py:30
  67.2 0.0 copy-start.1
  67.2 0.8 %copy-done.1 = f32[32,4,896]{2,1,0:T(4,128)} copy-done((f32[32,4,896]{2,1,0:T(4,128)}, f32[32,4,896]{2,1,0:T(4,128)S(1)}, u32[]{:S(2)}) %copy-start.1) | copy-done | bytes 458776
  68.0 5.0 %tail.1 = f32[50,2,256]{2,1,0:T(2,128)} custom-call(f32[32,4,896]{2,1,0:T(4,128)} %copy-done.1, f32[50,2,256]{2,1,0:T(2,128)} %bitcast.16, f32[50,50,256]{2,1,0:T(8,128)} %blocks_ref.1, s32[1,256]{1,0:T(1,128)} %order_ref.1, f32[2,256]{1,0:T(2,128)} %coef_ref.1, f32[2,50,50]{2,1,0:T(8,128)} %copy.17.faces_ref, s32[512,1]{1,0:T(8,128)} %copy.18.layers_ref, ...), custom_call_target="tpu_custom_call" | custom-call | tf_op jit(solution)/shard_map/tail/pallas_call | solution.py:163
  (7 shorter events, 0.2 us)
Async XLA Ops:
  0.0 57.8 %copy-start = (f32[384,384]{1,0:T(8,128)S(1)}, f32[384,384]{1,0:T(8,128)}, u32[]{:S(2)}) copy-start(f32[384,384]{1,0:T(8,128)} %param.19) | copy-start | bytes 1769476
  0.0 56.3 %copy-start.4 = (s32[1,4,128]{2,1,0:T(4,128)S(1)}, s32[1,4,128]{2,1,0:T(4,128)}, u32[]{:S(2)}) copy-start(s32[1,4,128]{2,1,0:T(4,128)} %param.15) | copy-start | bytes 6148
  0.0 57.1 %copy-start.3 = (f32[2,50,50]{2,0,1:T(2,128)S(1)}, f32[2,50,50]{2,0,1:T(2,128)}, u32[]{:S(2)}) copy-start(f32[2,50,50]{2,0,1:T(2,128)} %param.14) | copy-start | bytes 60004
  0.0 57.8 %copy-start.2 = (f32[256,384]{1,0:T(8,128)S(1)}, f32[256,384]{1,0:T(8,128)}, u32[]{:S(2)}) copy-start(f32[256,384]{1,0:T(8,128)} %modes_ref.1) | copy-start | bytes 1179652
  2.3 21.3 %all-to-all-start = ((f32[32,4,896]{2,1,0:T(4,128)}), f32[32,4,896]{2,1,0:T(4,128)S(1)}, u32[]{:S(2)}, u32[]{:S(2)}) async-start(f32[32,4,896]{2,1,0:T(4,128)} %front.1), calls=%async_computation | async-start | bytes 917504 | tf_op jit(solution)/shard_map/all_to_all | solution.py:30
  24.4 24.9 %all-to-all-start.1 = ((f32[16,4,384]{2,1,0:T(4,128)}), f32[16,4,384]{2,1,0:T(4,128)S(1)}, u32[]{:S(2)}, u32[]{:S(2)}) async-start(f32[16,4,384]{2,1,0:T(4,128)} %broadcast_in_dim.10), calls=%async_computation.1 | async-start | bytes 196608 | tf_op jit(solution)/shard_map/all_to_all | solution.py:30
  50.1 17.1 %all-to-all-start.2 = ((f32[32,4,896]{2,1,0:T(4,128)}), f32[32,4,896]{2,1,0:T(4,128)S(1)}, u32[]{:S(2)}, u32[]{:S(2)}) async-start(f32[32,4,896]{2,1,0:T(4,128)} %broadcast_dynamic-update-slice_fusion), calls=%async_computation.2 | async-start | bytes 917504 | tf_op jit(solution)/shard_map/all_to_all | solution.py:30
  67.2 0.8 %copy-start.1 = (f32[32,4,896]{2,1,0:T(4,128)}, f32[32,4,896]{2,1,0:T(4,128)S(1)}, u32[]{:S(2)}) copy-start(f32[32,4,896]{2,1,0:T(4,128)S(1)} %all-to-all-done.2.in_ref) | copy-start | bytes 1376260

commit v3 on v2

v3 whole, which is shorter than its diff:
```python
import jax
import jax.numpy as jnp
import numpy as np
from jax import lax
from jax.experimental import pallas as pl
from jax.experimental.pallas import tpu as pltpu
from jax.sharding import PartitionSpec as P


LINE = 32
ALL = ("wide", "narrow")
PLANE = 32
RING = 16
ROWS = 4
PAD = 56
BLOCKS = 2 * PAD // ROWS
F32 = jnp.float32
BF16 = jnp.bfloat16
GRANT = 16 << 20


def groups():
    place = np.arange(PLANE * RING).reshape(2, PLANE, 8)
    plane = place.transpose(0, 2, 1).reshape(-1, PLANE).tolist()
    ring = place.transpose(1, 0, 2).reshape(-1, RING).tolist()
    return plane, ring


def swap(blocks, groups_of):
    return lax.all_to_all(blocks, ALL, 0, 0, axis_index_groups=groups_of)


def partner(block, colour):
    count = lax.axis_size("wide")
    return lax.ppermute(block, "wide", [(i, i ^ 1 << colour) for i in range(count)])


def halves(x):
    high = x.astype(BF16)
    return high, (x - high.astype(F32)).astype(BF16)


def mul(a, b):
    return jnp.dot(a, b, preferred_element_type=F32)


def product(a, b):
    ah, al = halves(a)
    bh, bl = halves(b)
    n = a.shape[0]
    both = mul(jnp.concatenate([ah, al], axis=0), bh)
    return both[:n] + both[n:] + mul(ah, bl)


def choose(a, hit):
    ah, al = halves(a)
    n = a.shape[0]
    both = mul(jnp.concatenate([ah, al], axis=0), hit)
    return both[:n] + both[n:]


def one_hot(flags):
    return jnp.where(flags, 1.0, 0.0).astype(BF16)


def near(x):
    return pltpu.with_memory_space_constraint(x, pltpu.VMEM)


def far(*arrays):
    return [pltpu.with_memory_space_constraint(x, pltpu.HBM) for x in arrays]


def picks(layers_ref, count):
    ids = lax.broadcasted_iota(jnp.int32, (count, layers_ref.shape[1]), 0)
    return [one_hot(ids == layers_ref[c : c + 1, :]) for c in range(layers_ref.shape[0])]


def choose_back(a, hit):
    n = a.shape[0]
    both = jnp.concatenate(halves(a), axis=0)
    both = lax.dot_general(both, hit, (((1,), (1,)), ((), ())), preferred_element_type=F32)
    return both[:n] + both[n:]


def load_rows(x_ref, stack):
    ndof = x_ref.shape[0]
    stack[...] = jnp.zeros_like(stack)
    for app in range(2):
        stack[PAD * app : PAD * app + ndof, :] = x_ref[:, app, :]
    return stack[...]


def coarse_kernel(x_ref, modes_ref, out_ref, stack, wide):
    wide[...] = product(load_rows(x_ref, stack), modes_ref[...])
    for k in range(BLOCKS):
        out_ref[k] = wide[ROWS * k : ROWS * k + ROWS, :]
    for k in range(BLOCKS, PLANE):
        out_ref[k] = jnp.zeros(out_ref.shape[1:], F32)


def coarse_part(x3, modes):
    kc = modes.shape[1]
    return pl.pallas_call(
        coarse_kernel,
        out_shape=jax.ShapeDtypeStruct((PLANE, ROWS, kc), F32),
        scratch_shapes=[pltpu.VMEM((2 * PAD, x3.shape[2]), F32), pltpu.VMEM((2 * PAD, kc), F32)],
        compiler_params=pltpu.CompilerParams(vmem_limit_bytes=GRANT),
        name="coarse",
    )(*far(x3, modes))


def layer_kernel(x_ref, layers_ref, *rest):
    *outs, stack = rest
    x = load_rows(x_ref, stack)
    for out_ref, hit in zip(outs, picks(layers_ref, x.shape[1])):
        out_ref[...] = choose(x, hit)


def layer_parts(x3, layers):
    colours, span = layers.shape
    return pl.pallas_call(
        layer_kernel,
        out_shape=[jax.ShapeDtypeStruct((2 * PAD, span), F32)] * colours,
        scratch_shapes=[pltpu.VMEM((2 * PAD, x3.shape[2]), F32)],
        compiler_params=pltpu.CompilerParams(vmem_limit_bytes=GRANT),
        name="layers",
    )(*far(x3, layers))


def solve(blocks_ref, x):
    ndof, _, count = blocks_ref.shape
    rows = []
    for i in range(ndof):
        block = blocks_ref[i]
        left = jnp.sum(block * x[:, :count], axis=0, keepdims=True)
        right = jnp.sum(block * x[:, count:], axis=0, keepdims=True)
        rows.append(jnp.concatenate([left, right], axis=1))
    return jnp.concatenate(rows, axis=0)


def local_kernel(
    r0_ref, r1_ref, r2_ref, r3_ref, x_ref, blocks_hbm, order_ref, coef_ref, faces_ref, layers_ref, weights_ref,
    ghost_ref, out_ref, stack, blocks_ref, arrival,
):
    fetch = pltpu.make_async_copy(blocks_hbm, blocks_ref, arrival)
    fetch.start()
    ndof, _, count = x_ref.shape
    x = load_rows(x_ref, stack)
    span = layers_ref.size
    received = jnp.concatenate(
        [r_ref[PAD * a : PAD * a + ndof, :] for a in range(2) for r_ref in (r0_ref, r1_ref, r2_ref, r3_ref)], axis=1
    )
    pushed = product(ghost_ref[...], received)
    weights = weights_ref[...]
    zero = jnp.zeros((PAD - ndof, span), F32)
    pushed = jnp.concatenate(
        [pushed[:, :span] * weights, zero, pushed[:, span:] * weights, zero], axis=0
    )
    order = order_ref[...]
    hit = one_hot(lax.broadcasted_iota(jnp.int32, (count, count), 0) == order)
    boosted = x + choose_back(pushed, jnp.concatenate(picks(layers_ref, count), axis=1))
    ordered = choose(boosted, hit)
    ordered = jnp.concatenate([ordered[:ndof], ordered[PAD : PAD + ndof]], axis=1)
    fetch.wait()
    first = solve(blocks_ref, ordered)
    spot = lax.broadcasted_iota(jnp.int32, (1, count), 1) % LINE
    before = jnp.where(spot > 0, coef_ref[0:1, :], 0.0)
    after = jnp.where(spot < LINE - 1, coef_ref[1:2, :], 0.0)
    ahead = product(faces_ref[:, 0, :], first)
    behind = product(faces_ref[:, 1, :], first)
    coupled = []
    for a in range(2):
        cut = slice(a * count, a * count + count)
        coupled.append(
            ordered[:, cut]
            + before * pltpu.roll(ahead[:, cut], 1, 1)
            + after * pltpu.roll(behind[:, cut], count - 1, 1)
        )
    second = solve(blocks_ref, jnp.concatenate(coupled, axis=1))
    hole = jnp.zeros((PAD - ndof, count), F32)
    second = jnp.concatenate([second[:, :count], hole, second[:, count:], hole], axis=0)
    out_ref[...] = choose_back(second, hit)


def local_part(received, x3, blocks, order, coef, faces, layers, weights, ghost):
    count = x3.shape[2]
    near_spec = pl.BlockSpec(memory_space=pltpu.VMEM)
    return pl.pallas_call(
        local_kernel,
        out_shape=jax.ShapeDtypeStruct((2 * PAD, count), F32),
        in_specs=[near_spec] * 5 + [pl.BlockSpec(memory_space=pltpu.HBM)] + [near_spec] * 6,
        scratch_shapes=[
            pltpu.VMEM((2 * PAD, count), F32),
            pltpu.VMEM(blocks.shape, F32),
            pltpu.SemaphoreType.DMA(()),
        ],
        compiler_params=pltpu.CompilerParams(vmem_limit_bytes=GRANT),
        name="local",
    )(*map(near, received), *far(x3, blocks, order, coef, faces, layers, weights, ghost))


def lift_kernel(inv_ref, modes_ref, high_ref, low_ref):
    ah, al = halves(inv_ref[...])
    bh, bl = halves(modes_ref[...])
    turn = (((1,), (1,)), ((), ()))
    by = lambda u, v: lax.dot_general(u, v, turn, preferred_element_type=F32)
    high_ref[...], low_ref[...] = halves(by(ah, bh) + by(al, bh) + by(ah, bl))


def lift_part(coarse_inv, modes):
    shape = jax.ShapeDtypeStruct((modes.shape[1], modes.shape[0]), BF16)
    return pl.pallas_call(
        lift_kernel,
        out_shape=(shape, shape),
        compiler_params=pltpu.CompilerParams(vmem_limit_bytes=GRANT),
        name="lift",
    )(*far(coarse_inv, modes))


def last_kernel(coarse_ref, local_ref, high_ref, low_ref, out_ref, stack):
    ndof = out_ref.shape[0]
    for k in range(BLOCKS):
        stack[ROWS * k : ROWS * k + ROWS, :] = coarse_ref[k]
    ah, al = halves(stack[...])
    both = mul(jnp.concatenate([ah, al], axis=0), high_ref[...])
    total = local_ref[...] + both[: 2 * PAD] + both[2 * PAD :] + mul(ah, low_ref[...])
    for a in range(2):
        out_ref[:, a, :] = total[PAD * a : PAD * a + ndof]


def last(coarse, local, high, low, ndof):
    return pl.pallas_call(
        last_kernel,
        out_shape=jax.ShapeDtypeStruct((ndof, 2, local.shape[1]), F32),
        scratch_shapes=[pltpu.VMEM((2 * PAD, coarse.shape[2]), F32)],
        compiler_params=pltpu.CompilerParams(vmem_limit_bytes=GRANT),
        name="last",
    )(near(coarse), near(local), near(high), near(low))


def shards(
    rhs,
    block_inv,
    line_order,
    line_coef,
    line_faces,
    intersection,
    intersection_coef,
    ghost_face,
    modes,
    coarse_inv,
):
    plane, ring = groups()
    kc = modes.shape[1]
    x3 = jnp.transpose(rhs, (1, 0, 2))
    in0 = swap(coarse_part(x3, modes), plane)
    sent = layer_parts(x3, intersection[0])
    received = []
    for colour, block in enumerate(sent):
        received.append(partner(block, colour))
    part = jnp.sum(in0, axis=0)
    in1 = swap(jnp.broadcast_to(part, (RING, ROWS, kc)), ring)
    coarse = jnp.sum(in1, axis=0)
    in2 = swap(jnp.broadcast_to(coarse, (PLANE, ROWS, kc)), plane)
    high, low = lift_part(coarse_inv, modes)
    local = local_part(
        received,
        x3,
        block_inv,
        line_order,
        line_coef,
        jnp.transpose(line_faces, (1, 0, 2)),
        intersection[0],
        intersection_coef.reshape(1, -1),
        ghost_face,
    )
    out = last(in2, local, high, low, rhs.shape[1])
    return jnp.transpose(out, (1, 0, 2))


def solution(mesh):
    in_specs = (
        P(None, None, ALL),
        P(None, None, ALL),
        P(ALL, None),
        P(None, ALL),
        P(),
        P(ALL, None, None),
        P(ALL, None, None),
        P(),
        P(ALL, None),
        P(),
    )
    out_specs = P(None, None, ALL)
    return jax.shard_map(shards, mesh=mesh, in_specs=in_specs, out_specs=out_specs, check_vma=False)
```

time: 73.4 us -> 73.7 us (level)
  blocking collectives: 0 us -> 43.3 us
  waiting for transfers between devices: 27.3 us -> 0.08 us
  starting transfers between devices: 29.6 us -> 19.1 us
  local copies, waits for them, and re-layouts: 7.05 us -> 0.71 us
  Pallas kernels: 7.33 us -> 9.61 us
  matrix products: 1.53 us -> 0 us
    all_to_all x0 -> x2, blocking collectives: none -> 43.3 us  [swap(): return lax.all_to_all(blocks, ALL, 0, 0, axis_index_groups=groups_of)]
    all_to_all x3 -> x1, waiting for transfers between devices: 27.3 us -> 0.01 us  [swap(): return lax.all_to_all(blocks, ALL, 0, 0, axis_index_groups=groups_of)]
    all_to_all x3 -> x1, starting transfers between devices: 29.6 us -> 6.04 us  [swap(): return lax.all_to_all(blocks, ALL, 0, 0, axis_index_groups=groups_of)]
    ppermute x0 -> x4, starting transfers between devices: none -> 13 us  [partner(): lax.ppermute(block, 'wide', [(i, i ^ 1 << colour) for i in range(count)])]
    unnamed x15 -> x0, local copies, waits for them, and re-layouts: 4.08 us -> none
    pallas_call x2 -> x5, Pallas kernels: 7.33 us -> 9.61 us  [the longest x1 4.54 us: local_part(): pl.pallas_call(local_kernel, out_shape=jax.ShapeDtypeStruct((2 * PAD, cou...]
    dot_general x1 -> x0, matrix products: 1.53 us -> none  [shards(): lift = jnp.dot(coarse_inv, modes.T, precision=HI)]
    reshape x1 -> x0, local copies, waits for them, and re-layouts: 0.85 us -> none  [shards(): intersection.reshape(-1, 1)]
  transfers between devices with their start and end apart: 3 -> 5, of which waited for: 3 -> 1; matrix products, arithmetic and copies ran while one was open for 9% -> 0% of each run, Pallas kernels for 0% -> 10%
where the time goes in v3:
time: 73.7 us; the launch traced here: 72.9 us
  blocking collectives  43.3 us (59%)
  starting transfers between devices  19.1 us (26%)
  Pallas kernels  9.61 us (13%)
    all_to_all x2, blocking collectives, swap(): return lax.all_to_all(blocks, ALL, 0, 0, axis_index_groups=groups_of)  43.3 us
    ppermute x4, starting transfers between devices, partner(): lax.ppermute(block, 'wide', [(i, i ^ 1 << colour) for i in range(count)])  13 us
    all_to_all x1, starting transfers between devices, swap(): return lax.all_to_all(blocks, ALL, 0, 0, axis_index_groups=groups_of)  6.04 us
    pallas_call x1, Pallas kernels, local_part(): pl.pallas_call(local_kernel, out_shape=jax.ShapeDtypeStruct((2 * PAD, cou...  4.54 us
    pallas_call x1, Pallas kernels, lift_part(): pl.pallas_call(lift_kernel, out_shape=(shape, shape), compiler_params=plt...  1.66 us
  transfers between devices with their start and end apart: 5, of which 1 were waited for; matrix products, arithmetic and copies ran while one was open for 0% of the time, Pallas kernels for 10%

profile of v3, /device:TPU:1, one launch (start us, length us, event | category | flops | bytes accessed | tf_op | source)
XLA Modules:
  0.0 72.9 jit_solution(1021932451633678992)
XLA Ops:
  0.0 1.3 %coarse.1 = f32[32,4,384]{2,1,0:T(4,128)S(1)} custom-call(f32[50,2,256]{2,1,0:T(2,128)} %bitcast.5, f32[256,384]{1,0:T(8,128)} %modes_ref.3), custom_call_target="tpu_custom_call" | custom-call | tf_op jit(solution)/shard_map/coarse/pallas_call | solution.py:104
  1.3 17.8 %all_to_all.15 = f32[32,4,384]{2,1,0:T(4,128)S(1)} all-to-all(f32[32,4,384]{2,1,0:T(4,128)S(1)} %coarse.1), channel_id=1, replica_groups={{0,8,16,24,32,40,48,56,64,72,80,88,96,104,112,120,128,136,144,152,160,1..., dimensions={0} | all-to-all | bytes 393216 | tf_op jit(solution)/shard_map/all_to_all | solution.py:30
  19.1 0.1 reduce_sum.18
  19.2 25.4 %all_to_all.16 = f32[16,4,384]{2,1,0:T(4,128)S(1)} all-to-all(f32[16,4,384]{2,1,0:T(4,128)S(1)} %broadcast_in_dim.6), channel_id=1, replica_groups={{0,1,2,3,4,5,6,7,256,257,258,259,260,261,262,263},{8,9,10,11,12,13,14,1..., dimensions={0} | all-to-all | bytes 196608 | tf_op jit(solution)/shard_map/all_to_all | solution.py:30
  44.7 0.7 broadcast_in_dim.7
  45.4 6.0 %all-to-all-start.2 = ((f32[32,4,384]{2,1,0:T(4,128)}), f32[32,4,384]{2,1,0:T(4,128)S(1)}, u32[]{:S(2)}, u32[]{:S(2)}) async-start(f32[32,4,384]{2,1,0:T(4,128)} %broadcast_in_dim.7), calls=%async_computation.2 | async-start | bytes 393216 | tf_op jit(solution)/shard_map/all_to_all | solution.py:30
  51.4 1.2 %layers.1 = (f32[112,128]{1,0:T(8,128)S(1)}, f32[112,128]{1,0:T(8,128)S(1)}, f32[112,128]{1,0:T(8,128)S(1)}, f32[112,128]{1,0:T(8,128)S(1)}) custom-call(f32[50,2,256]{2,1,0:T(2,128)} %bitcast.6, s32[4,128]{1,0:T(4,128)} %bitcast.9), custom_call_target="tpu_custom_call" | custom-call | tf_op jit(solution)/shard_map/layers/pallas_call | solution.py:122
  52.6 2.3 %collective-permute-start = (f32[112,128]{1,0:T(8,128)S(1)}, f32[112,128]{1,0:T(8,128)S(1)}, u32[]{:S(2)}, u32[]{:S(2)}) collective-permute-start(f32[112,128]{1,0:T(8,128)S(1)} %get-tuple-element.11), channel_id=1, source_target_pairs={{0,8},{8,0},{16,24},{24,16},{32,40},{40,32},{48,56},{56,48},{64,72... | collective-permute-start | bytes 172040 | tf_op jit(solution)/shard_map/ppermute | solution.py:35
  54.9 3.3 %collective-permute-start.1 = (f32[112,128]{1,0:T(8,128)S(1)}, f32[112,128]{1,0:T(8,128)S(1)}, u32[]{:S(2)}, u32[]{:S(2)}) collective-permute-start(f32[112,128]{1,0:T(8,128)S(1)} %get-tuple-element.12), channel_id=1, source_target_pairs={{0,16},{8,24},{16,0},{24,8},{32,48},{40,56},{48,32},{56,40},{64,80... | collective-permute-start | bytes 172040 | tf_op jit(solution)/shard_map/ppermute | solution.py:35
  58.2 4.3 %collective-permute-start.2 = (f32[112,128]{1,0:T(8,128)S(1)}, f32[112,128]{1,0:T(8,128)S(1)}, u32[]{:S(2)}, u32[]{:S(2)}) collective-permute-start(f32[112,128]{1,0:T(8,128)S(1)} %get-tuple-element.13), channel_id=1, source_target_pairs={{0,32},{8,40},{16,48},{24,56},{32,0},{40,8},{48,16},{56,24},{64,96... | collective-permute-start | bytes 172040 | tf_op jit(solution)/shard_map/ppermute | solution.py:35
  62.5 3.1 %collective-permute-start.3 = (f32[112,128]{1,0:T(8,128)S(1)}, f32[112,128]{1,0:T(8,128)S(1)}, u32[]{:S(2)}, u32[]{:S(2)}) collective-permute-start(f32[112,128]{1,0:T(8,128)S(1)} %get-tuple-element.14), channel_id=1, source_target_pairs={{0,64},{8,72},{16,80},{24,88},{32,96},{40,104},{48,112},{56,120},{... | collective-permute-start | bytes 172040 | tf_op jit(solution)/shard_map/ppermute | solution.py:35
  65.7 1.7 %lift.1 = (bf16[384,256]{1,0:T(8,128)(2,1)S(1)}, bf16[384,256]{1,0:T(8,128)(2,1)S(1)}) custom-call(f32[384,384]{1,0:T(8,128)} %inv_ref.1, f32[256,384]{1,0:T(8,128)} %modes_ref.3), custom_call_target="tpu_custom_call" | custom-call | tf_op jit(solution)/shard_map/lift/pallas_call | solution.py:213
  67.4 0.0 collective-permute-done.r0_ref
  67.4 0.0 collective-permute-done.1.r1_ref
  67.4 0.0 collective-permute-done.2.r2_ref
  67.4 0.1 collective-permute-done.3.r3_ref
  67.5 4.5 %local.1.local_ref = f32[112,256]{1,0:T(8,128)S(1)} custom-call(f32[112,128]{1,0:T(8,128)S(1)} %collective-permute-done.r0_ref, f32[112,128]{1,0:T(8,128)S(1)} %collective-permute-done.1.r1_ref, f32[112,128]{1,0:T(8,128)S(1)} %collective-permute-done.2.r2_ref, f32[112,128]{1,0:T(8,128)S(1)} %collective-permute-done.3.r3_ref, f32[50,2,256]{2,1,0:T(2,128)} %bitcast.7, ...), custom_call_target="tpu_custom_call" | custom-call | tf_op jit(solution)/shard_map/local/pallas_call | solution.py:189
  72.0 0.0 all-to-all-done.2.coarse_ref
  72.0 0.9 %last.1 = f32[50,2,256]{2,1,0:T(2,128)} custom-call(f32[32,4,384]{2,1,0:T(4,128)S(1)} %all-to-all-done.2.coarse_ref, f32[112,256]{1,0:T(8,128)S(1)} %local.1.local_ref, bf16[384,256]{1,0:T(8,128)(2,1)S(1)} %get-tuple-element.15.high_ref, bf16[384,256]{1,0:T(8,128)(2,1)S(1)} %get-tuple-element.16.low_ref), custom_call_target="tpu_custom_call" | custom-call | tf_op jit(solution)/shard_map/last/pallas_call | solution.py:233
  (2 shorter events, 0.1 us)
Async XLA Ops:
  45.4 26.6 %all-to-all-start.2 = ((f32[32,4,384]{2,1,0:T(4,128)}), f32[32,4,384]{2,1,0:T(4,128)S(1)}, u32[]{:S(2)}, u32[]{:S(2)}) async-start(f32[32,4,384]{2,1,0:T(4,128)} %broadcast_in_dim.7), calls=%async_computation.2 | async-start | bytes 393216 | tf_op jit(solution)/shard_map/all_to_all | solution.py:30
  52.6 14.7 %collective-permute-start = (f32[112,128]{1,0:T(8,128)S(1)}, f32[112,128]{1,0:T(8,128)S(1)}, u32[]{:S(2)}, u32[]{:S(2)}) collective-permute-start(f32[112,128]{1,0:T(8,128)S(1)} %get-tuple-element.11), channel_id=1, source_target_pairs={{0,8},{8,0},{16,24},{24,16},{32,40},{40,32},{48,56},{56,48},{64,72... | collective-permute-start | bytes 172040 | tf_op jit(solution)/shard_map/ppermute | solution.py:35
  54.9 12.5 %collective-permute-start.1 = (f32[112,128]{1,0:T(8,128)S(1)}, f32[112,128]{1,0:T(8,128)S(1)}, u32[]{:S(2)}, u32[]{:S(2)}) collective-permute-start(f32[112,128]{1,0:T(8,128)S(1)} %get-tuple-element.12), channel_id=1, source_target_pairs={{0,16},{8,24},{16,0},{24,8},{32,48},{40,56},{48,32},{56,40},{64,80... | collective-permute-start | bytes 172040 | tf_op jit(solution)/shard_map/ppermute | solution.py:35
  58.2 9.2 %collective-permute-start.2 = (f32[112,128]{1,0:T(8,128)S(1)}, f32[112,128]{1,0:T(8,128)S(1)}, u32[]{:S(2)}, u32[]{:S(2)}) collective-permute-start(f32[112,128]{1,0:T(8,128)S(1)} %get-tuple-element.13), channel_id=1, source_target_pairs={{0,32},{8,40},{16,48},{24,56},{32,0},{40,8},{48,16},{56,24},{64,96... | collective-permute-start | bytes 172040 | tf_op jit(solution)/shard_map/ppermute | solution.py:35
  62.5 4.9 %collective-permute-start.3 = (f32[112,128]{1,0:T(8,128)S(1)}, f32[112,128]{1,0:T(8,128)S(1)}, u32[]{:S(2)}, u32[]{:S(2)}) collective-permute-start(f32[112,128]{1,0:T(8,128)S(1)} %get-tuple-element.14), channel_id=1, source_target_pairs={{0,64},{8,72},{16,80},{24,88},{32,96},{40,104},{48,112},{56,120},{... | collective-permute-start | bytes 172040 | tf_op jit(solution)/shard_map/ppermute | solution.py:35
